TPU v7x, 256 devices: a whole 4x4x8 slice. The times are simulated.
256 devices in a mesh: pb: 16 (over x_lo, z), ka: 8 (over y, core), ha: 2 (over x_hi).
Axes of the slice: x: 4 (x_hi: 2, x_lo: 2; x = x_hi * 2 + x_lo), y: 4, z: 8, core: 2. Of those that a mesh axis runs over, the one named last changes fastest.
Arguments:
- queries: bfloat16 [16384, 4096], P('pb', 'ha'), may hold values from -512 to 512
- keys: bfloat16 [16, 8, 128, 512], P('pb', 'ka', None, 'ha'), may hold values from -6 to 6
- values: bfloat16 [16, 8, 128, 512], P('pb', 'ka', None, 'ha'), may hold values from -6 to 6
- q_order: int32 [128], P('pb'), may hold values from 0 to 127, as said below
- block_mask: int32 [128, 128], P('pb'), may hold values from 0 to 1, as said below
Outputs:
- attended: bfloat16 [16384, 4096], P(('pb', 'ka'), 'ha')
Inputs may be any that keep to these rules, and one draw needn't show every extreme that they name: `q_order`: slots 2m and 2m+1 hold query blocks i and 127 - i for some i, in either order; every block sits in exactly one slot. block_mask[s, b] is 1 only where b <= q_order[s], and block_mask[s, q_order[s]] is 1. For every m and every r below 8, slots 2m and 2m+1 together list at most 8 key blocks b with b % 8 == r, and exactly 8 for some m and r in every draw.
All inputs are finite; a program needn't handle non-finite values.
Results may differ from a plain program's by a relative error of at most 0.0042.
Values may be sent and summed in bfloat16 or wider, within the bound.
A program may use at most 128 MiB of HBM per device.

v0:
```python
import functools
import math

import jax
import jax.numpy as jnp
from jax import lax
from jax.experimental import pallas as pl
from jax.experimental.pallas import tpu as pltpu
from jax.sharding import PartitionSpec as P

MESH = pl.DeviceIdType.MESH
K, V = 0, 1
BF16, F32, I32 = jnp.bfloat16, jnp.float32, jnp.int32
D = 128
GROUP = 8
LANES = GROUP * D
RING = 8
POOL = 64
NG = 9
WIDE = 4
SCALE = math.log2(math.e) / math.sqrt(D)
LOW = -1e30
VMEM_LIMIT = 60 * 1024 * 1024


def head_of(y):
    return lax.rem(lax.div(y + 1, 2), 2)


def gather(k_ref, v_ref, kbuf, vbuf, send, recv, local, meanwhile, later):
    pb, ka = lax.axis_index("pb"), lax.axis_index("ka")
    x, z = lax.div(pb, RING), lax.rem(pb, RING)
    y, c = lax.div(ka, 2), lax.rem(ka, 2)
    u = lax.rem(y, 2)
    mate = {"ka": (y + 1 - 2 * u) * 2 + c}
    across = {"pb": (1 - x) * RING + z}
    up = {"pb": x * RING + lax.rem(z + 1, RING)}
    down = {"pb": x * RING + lax.rem(z + RING - 1, RING)}
    sibling = {"ka": y * 2 + 1 - c}
    corner = {"pb": (1 - x) * RING + z, "ka": (y + 1 - 2 * u) * 2 + c}
    head = head_of(y)

    started = []
    number = [0]

    def next_id():
        number[0] += 1
        return number[0] - 1

    def move(src, dst, landed, who):
        n = next_id()
        copy = pltpu.make_async_remote_copy(
            src_ref=src, dst_ref=dst, send_sem=send.at[n], recv_sem=recv.at[n],
            device_id=who, device_id_type=MESH,
        )
        copy.start()
        started.append(copy)
        return pltpu.make_async_remote_copy(
            src_ref=src, dst_ref=landed, send_sem=send.at[n], recv_sem=recv.at[n],
            device_id=who, device_id_type=MESH,
        )

    def ring(s):
        return lax.rem(z + s + RING, RING)

    def spot(core, zz, uu, xx):
        return ((core * RING + zz) * 2 + uu) * 2 + xx

    late = []

    def blocks(buf, at, count):
        return buf.at[pl.ds(at, count)]

    def same(buf, at, count, who, landed):
        return move(blocks(buf, at, count), blocks(buf, at, count), blocks(buf, landed, count), who)

    def to_sibling(buf, at, count):
        late.append(same(buf, at, count, sibling, at + (1 - 2 * c) * (POOL // 2)))

    own_u, new_u = u, 1 - u
    own, new = spot(c, z, own_u, x), spot(c, z, new_u, x)
    ours = pl.ds(pl.multiple_of(head * D, D), D)
    theirs = pl.ds(pl.multiple_of((1 - head) * D, D), D)
    k_swap = move(k_ref.at[:, theirs], kbuf.at[own], kbuf.at[new], mate)
    v_swap = move(v_ref.at[:, theirs], vbuf.at[own], vbuf.at[new], mate)
    k_cross = move(k_ref.at[:, ours], kbuf.at[own], kbuf.at[spot(c, z, own_u, 1 - x)], across)
    k_diagonal = move(k_ref.at[:, theirs], kbuf.at[own], kbuf.at[spot(c, z, new_u, 1 - x)], corner)
    v_up = [move(v_ref.at[:, ours], vbuf.at[own], vbuf.at[spot(c, ring(-1), own_u, x)], up)]
    v_down = [move(v_ref.at[:, ours], vbuf.at[own], vbuf.at[spot(c, ring(1), own_u, x)], down)]
    v_cross = [(z, own_u, move(v_ref.at[:, ours], vbuf.at[own], vbuf.at[spot(c, z, own_u, 1 - x)], across))]
    mine = [
        pltpu.make_async_copy(r.at[:, ours], b.at[own], local.at[i])
        for i, (r, b) in enumerate(((k_ref, kbuf), (v_ref, vbuf)))
    ]
    for copy in mine:
        copy.start()
    meanwhile()
    for copy in mine:
        copy.wait()

    def cross_v(zz, uu):
        at, landed = spot(c, zz, uu, x), spot(c, zz, uu, 1 - x)
        v_cross.append((zz, uu, same(vbuf, at, 1, across, landed)))

    def land_v():
        zz, uu, copy = v_cross.pop(0)
        copy.wait_recv()
        to_sibling(vbuf, spot(c, zz, uu, 0), 2)

    units = (own_u, new_u)

    def pass_on(kind, i, zz, who, landed):
        if kind == K:
            return same(kbuf, spot(c, zz, units[i], 0), 2, who, spot(c, landed, units[i], 0))
        return same(vbuf, spot(c, zz, units[i], x), 1, who, spot(c, landed, units[i], x))

    coming = {(V, 0): (v_up[0], v_down[0])}

    def begin(kind, i):
        coming[kind, i] = (pass_on(kind, i, z, up, ring(-1)), pass_on(kind, i, z, down, ring(1)))

    def advance(kind, i, s):
        from_below, from_above = coming.pop((kind, i))
        lo, hi = ring(-s), ring(s)
        goes_up, goes_down = s < 3 or (s == 3 and i == 0), s < 3 or (s == 3 and i == 1)
        upward = downward = None
        got = []
        if from_below is not None:
            from_below.wait_recv()
            got.append(lo)
            if goes_up:
                upward = pass_on(kind, i, lo, up, ring(-s - 1))
        if from_above is not None:
            from_above.wait_recv()
            got.append(hi)
            if goes_down:
                downward = pass_on(kind, i, hi, down, ring(s + 1))
        coming[kind, i] = (upward, downward)
        for zz in got:
            if kind == K:
                to_sibling(kbuf, spot(c, zz, units[i], 0), 2)
            else:
                cross_v(zz, units[i])

    k_cross.wait_recv()
    begin(K, 0)
    v_swap.wait_recv()
    begin(V, 1)
    cross_v(z, new_u)
    k_swap.wait_recv()
    advance(V, 0, 1)
    later()
    k_diagonal.wait_recv()
    begin(K, 1)
    to_sibling(kbuf, spot(c, z, 0, 0), 4)
    order = ((K, 0, 1), (V, 1, 1), (V, 0, 2), (K, 1, 1), (K, 0, 2), (V, 1, 2), (V, 0, 3), (K, 1, 2), (K, 0, 3), (V, 1, 3),
             (V, 0, 4), (K, 1, 3), (K, 0, 4), (V, 1, 4), (K, 1, 4))
    for kind, i, s in order:
        advance(kind, i, s)
        while len(v_cross) > 4:
            land_v()
    while v_cross:
        land_v()
    for copy in late:
        copy.wait_recv()
    for copy in started:
        copy.wait_send()


COPIES = 80


HALF = 512
CHUNK = 256
EXTRA = 16
UNROLL = 7
ENTRIES = 40


def write_lists(order_ref, mask_ref, lvm, rows, group):
    lane = lax.broadcasted_iota(I32, (8, D), 1)
    slot = lax.broadcasted_iota(I32, (8, D), 0)
    mine = jnp.zeros((8, D), I32)
    for r in range(8):
        mine = jnp.where(slot == r, order_ref[r], mine)
    listed = jnp.logical_and(mask_ref[...] == 1, ((lane >> 2) & 1) == group)
    diagonal = lane == mine
    both = jnp.where(jnp.logical_and(listed, diagonal), 1, 0)
    rank = jnp.where(jnp.logical_and(listed, jnp.logical_not(diagonal)), 1, 0)
    total, has = rank, both
    for k in (1, 2, 4, 8, 16, 32, 64):
        rank = rank + jnp.where(lane >= k, pltpu.roll(rank, k, 1), 0)
        total = total + pltpu.roll(total, k, 1)
        has = has + pltpu.roll(has, k, 1)
    front = jnp.where(diagonal, 0, rank - 1 + has)
    back = jnp.where(diagonal, WIDE * NG - 1, WIDE * NG - rank - has)
    at = jnp.where(listed, jnp.where((slot & 1) == 0, front, back), -1)
    spot = (lane & 1) * 32 + ((lane >> 3) & 7) * 4 + ((lane >> 1) & 1) * 2 + (lane >> 6)
    rows[0] = at
    rows[1] = spot + POOL * jnp.where(diagonal, 1, 0) - 2 * POOL
    rows[2] = jnp.maximum((total + has + WIDE - 1) >> 2, 1)
    place = lax.broadcasted_iota(I32, (ENTRIES, D), 0)
    for p in range(4):
        found = jnp.zeros((ENTRIES, D), I32)
        for j in range(2):
            row = slice(2 * p + j, 2 * p + j + 1)
            found = found + jnp.where(place == rows[0, row], rows[1, row], 0)
        for k in (1, 2, 4, 8, 16, 32, 64):
            found = found + pltpu.roll(found, k, 1)
        first_groups = jnp.broadcast_to(rows[2, 2 * p:2 * p + 1], (ENTRIES, D))
        lvm[p] = jnp.where(place == ENTRIES - 1, first_groups, found + 2 * POOL)


def fused_kernel(order_ref, mask_ref, q_hbm, k_ref, v_ref, out_ref, lvm, table, lsm, kbuf, vbuf, qs, bias, acc, mb, sb, obuf, sbuf, land, lstat,
                 send, recv, local, lsem, qsem, xsend, xrecv, near_sem):
    pb, ka = lax.axis_index("pb"), lax.axis_index("ka")
    x, z = lax.div(pb, RING), lax.rem(pb, RING)
    y, c = lax.div(ka, 2), lax.rem(ka, 2)
    head = head_of(y)

    barrier = pltpu.get_barrier_semaphore()
    partners = [{"ka": lax.rem(ka + d, 8)} for d in range(1, 8)]
    partners += [
        {"pb": (1 - x) * RING + z},
        {"pb": (1 - x) * RING + z, "ka": (y + 1 - 2 * lax.rem(y, 2)) * 2 + c},
        {"pb": x * RING + lax.rem(z + 1, RING)},
        {"pb": x * RING + lax.rem(z + RING - 1, RING)},
    ]
    for who in partners:
        pl.semaphore_signal(barrier, inc=1, device_id=who, device_id_type=MESH)
    pl.semaphore_wait(barrier, len(partners))

    fetch = []
    fetch_lists = pltpu.make_async_copy(lvm, lsm, lsem)
    later = fetch_lists.start

    def meanwhile():
        write_lists(order_ref, mask_ref, lvm, table, lax.div(y, 2))
        for s in range(8):
            for i in range(HALF // D):
                cols = pl.ds(pl.multiple_of(head * LANES + c * HALF + i * D, D), D)
                copy = pltpu.make_async_copy(
                    q_hbm.at[pl.ds(s * D, D), cols], qs.at[s, pl.ds(i * D, D)], qsem.at[s * (HALF // D) + i]
                )
                copy.start()
                fetch.append(copy)
        row = lax.broadcasted_iota(I32, (D, D), 0)
        col = lax.broadcasted_iota(I32, (D, D), 1)
        bias[0] = jnp.zeros((D, D), F32)
        bias[1] = jnp.where(row <= col, 0.0, LOW)
        acc[0] = jnp.zeros(acc.shape[1:], F32)
        mb[0] = jnp.full(mb.shape[1:], LOW, F32)

    gather(k_ref, v_ref, kbuf, vbuf, send, recv, local, meanwhile, later)
    fetch_lists.wait()
    for copy in fetch:
        copy.wait()

    ones = jnp.where(lax.broadcasted_iota(I32, (EXTRA, WIDE * D), 0) == 0, 1.0, 0.0).astype(BF16)

    def entries(p, g):
        return [lsm[p, WIDE * g + k, 0] for k in range(WIDE)]

    def split(p):
        return lsm[p, ENTRIES - 1, 0]

    def scores(p, g, w):
        owner = (g >= split(p)).astype(I32)
        k = jnp.concatenate([kbuf[e & (POOL - 1)] for e in entries(p, g)], axis=0)
        q = qs[2 * p + owner, w:w + CHUNK, :]
        return lax.dot_general(k, q, (((1,), (1,)), ((), ())), preferred_element_type=F32)

    def stage(p, g, diagonal, more=True):
        listed = entries(p, g)
        first = jnp.logical_or(g == 0, g == split(p))
        pads = [e >= 2 * POOL for e in listed]
        v = jnp.concatenate([vbuf[e & (POOL - 1)] for e in listed], axis=0)
        vt = jnp.concatenate([v.T, ones], axis=0)
        now, then = lax.rem(jnp.int32(g), 2), lax.rem(jnp.int32(g) + 1, 2)
        for w in range(0, HALF, CHUNK):
            cut = slice(w, w + CHUNK)
            pieces = [sb[now, k * D:(k + 1) * D, cut] for k in range(WIDE)]
            if more:
                sb[then, :, cut] = scores(p, g + 1, w)
            if diagonal is not None:
                causal = bias[(listed[diagonal] >> 6) & 1]
                pieces[diagonal] = pieces[diagonal] + jnp.concatenate([causal] * (CHUNK // D), axis=1)
            old = jnp.where(first, -3e38, mb[g, 0:1, cut])
            m = old
            for s, pad in zip(pieces, pads):
                m = jnp.maximum(m, jnp.where(pad, LOW, jnp.max(s, axis=0, keepdims=True)))
            alpha = jnp.exp2((old - m) * SCALE)
            weights = [
                jnp.exp2((s - jnp.where(pad, -LOW, m)) * SCALE).astype(BF16) for s, pad in zip(pieces, pads)
            ]
            part = lax.dot_general(
                vt, jnp.concatenate(weights, axis=0), (((1,), (0,)), ((), ())), preferred_element_type=F32
            )
            acc[g + 1, :, cut] = acc[g, :, cut] * alpha + part
            mb[g + 1, 0:1, cut] = m

    odd = lax.rem(y, 2)
    nearby, far, partner = y + 1 - 2 * odd, lax.rem(y + 2, 4), 3 - y
    kinds = ((obuf, land), (sbuf, lstat))

    def part_to(phase, j, kind, target):
        src, dst = kinds[kind]
        n = 2 * phase + j
        return pltpu.make_async_remote_copy(
            src_ref=src.at[n], dst_ref=dst.at[y, c], send_sem=xsend.at[n, kind], recv_sem=xrecv.at[y, c, kind],
            device_id={"ka": target}, device_id_type=MESH,
        )

    def stays(kind):
        src, dst = kinds[kind]
        return pltpu.make_async_copy(src.at[6 + c], dst.at[y, c], near_sem.at[kind])

    def pair_of(phase):
        return jnp.where(phase == 0, far, jnp.where(phase == 1, nearby, jnp.where(phase == 2, partner, y)))

    def run_phase(phase, _):
        p = pair_of(phase)
        for w in range(0, HALF, CHUNK):
            sb[0, :, w:w + CHUNK] = scores(p, 0, w)
        stage(p, 0, 0)

        def step(i, _):
            for t in range(UNROLL):
                stage(p, 1 + i * UNROLL + t, None)
            return 0

        lax.fori_loop(0, (NG - 2) // UNROLL, step, 0)
        stage(p, NG - 1, WIDE - 1, more=False)
        for j in range(2):
            at = split(p) if j == 0 else NG
            obuf[2 * phase + j] = acc[at, 0:D].astype(BF16)
            sbuf[2 * phase + j, 0:1] = mb[at, 0:1]
            sbuf[2 * phase + j, 1:2] = acc[at, D:D + 1]
        for j in range(2):
            mine = jnp.logical_and(phase == 3, c == j)
            for kind in range(2):
                pl.when(jnp.logical_not(mine))(part_to(phase, j, kind, 2 * p + j).start)
                pl.when(mine)(stays(kind).start)
        return 0

    lax.fori_loop(0, 4, run_phase, 0)

    for kv, a, b in ((1 - head, nearby, far), (head, partner, y)):
        for core in range(2):
            for kind in range(2):
                dst = kinds[kind][1]
                for yy in (a, b):
                    come = pltpu.make_async_remote_copy(
                        src_ref=dst.at[yy, core], dst_ref=dst.at[yy, core], send_sem=xsend.at[0, kind],
                        recv_sem=xrecv.at[yy, core, kind], device_id={"ka": lax.rem(ka + 1, 8)}, device_id_type=MESH,
                    )
                    if yy is y:
                        pl.when(core != c)(come.wait_recv)
                        pl.when(core == c)(stays(kind).wait)
                    else:
                        come.wait_recv()
            ma, mb_ = lstat[a, core, 0:1], lstat[b, core, 0:1]
            top = jnp.maximum(ma, mb_)
            fa, fb = jnp.exp2((ma - top) * SCALE), jnp.exp2((mb_ - top) * SCALE)
            whole = fa * lstat[a, core, 1:2] + fb * lstat[b, core, 1:2]
            fa, fb = fa / whole, fb / whole
            for i in range(HALF // D):
                cut = slice(i * D, (i + 1) * D)
                both = land[a, core, :, cut].astype(F32) * fa[:, cut] + land[b, core, :, cut].astype(F32) * fb[:, cut]
                at = pl.multiple_of(kv * LANES + core * HALF + i * D, D)
                out_ref[:, pl.ds(at, D)] = both.T.astype(BF16)
    for phase in range(4):
        for j in range(2):
            for kind in range(2):
                copy = part_to(phase, j, kind, 2 * pair_of(phase) + j)
                if phase < 3:
                    copy.wait_send()
                else:
                    pl.when(c != j)(copy.wait_send)


def fused(q_order, block_mask, queries, keys, values):
    vmem = pl.BlockSpec(memory_space=pltpu.VMEM)
    smem = pl.BlockSpec(memory_space=pltpu.SMEM)
    dma = pltpu.SemaphoreType.DMA
    return pl.pallas_call(
        fused_kernel,
        out_shape=jax.ShapeDtypeStruct((D, 2 * LANES), BF16),
        in_specs=[smem, vmem, pl.BlockSpec(memory_space=pl.ANY), vmem, vmem],
        out_specs=vmem,
        scratch_shapes=[
            pltpu.VMEM((4, ENTRIES, D), I32),
            pltpu.VMEM((3, 8, D), I32),
            pltpu.SMEM((4, ENTRIES, D), I32),
            pltpu.VMEM((POOL, D, D), BF16),
            pltpu.VMEM((POOL, D, D), BF16),
            pltpu.VMEM((8, HALF, D), BF16),
            pltpu.VMEM((2, D, D), F32),
            pltpu.VMEM((NG + 1, D + EXTRA, HALF), F32),
            pltpu.VMEM((NG + 1, 8, HALF), F32),
            pltpu.VMEM((2, WIDE * D, HALF), F32),
            pltpu.VMEM((8, D, HALF), BF16),
            pltpu.VMEM((8, 8, HALF), F32),
            pltpu.VMEM((4, 2, D, HALF), BF16),
            pltpu.VMEM((4, 2, 8, HALF), F32),
            dma((COPIES,)), dma((COPIES,)), dma((2,)), dma(()), dma((8 * HALF // D,)),
            dma((8, 2)), dma((4, 2, 2)), dma((2,)),
        ],
        compiler_params=pltpu.CompilerParams(
            collective_id=0, has_side_effects=True, vmem_limit_bytes=VMEM_LIMIT,
        ),
        name="attend_all",
    )(q_order, block_mask, queries, keys, values)


def on_device(queries, keys, values, q_order, block_mask):
    return fused(q_order, block_mask, queries, keys.reshape(D, 2 * D), values.reshape(D, 2 * D))


def solution(mesh):
    in_specs = (P("pb", "ha"), P("pb", "ka", None, "ha"), P("pb", "ka", None, "ha"), P("pb"), P("pb", None))
    return jax.shard_map(
        on_device, mesh=mesh, in_specs=in_specs, out_specs=P(("pb", "ka"), "ha"), check_vma=False
    )
```

profile of v0, /device:TPU:1, one launch (start us, length us, event | category | flops | bytes accessed | tf_op | source)
XLA Modules:
  0.0 56.6 jit_solution(8539141788825064161)
XLA Ops:
  0.0 54.8 %attend_all.1 = bf16[128,2048]{1,0:T(8,128)(2,1)} custom-call(s32[8]{0:T(128)} %order_ref.1, s32[8,128]{1,0:T(8,128)} %mask_ref.1, bf16[1024,2048]{1,0:T(8,128)(2,1)} %q_hbm.1, bf16[128,256]{1,0:T(8,128)(2,1)} %bitcast.2, bf16[128,256]{1,0:T(8,128)(2,1)} %bitcast.3), custom_call_target="tpu_custom_call" | custom-call | tf_op jit(solution)/shard_map/attend_all/pallas_call | solution.py:386
  54.8 1.9 %copy.7 = bf16[128,2048]{1,0:T(8,128)(2,1)} copy(bf16[128,2048]{1,0:T(8,128)(2,1)} %attend_all.1) | data formatting | bytes 1048576
where the time goes:
time: 56.8 us; the launch traced here: 56.6 us
  Pallas kernels  54.8 us (96%)
  local copies, waits for them, and re-layouts  1.88 us (3%)
    pallas_call x1, Pallas kernels, fused(): pl.pallas_call(fused_kernel, out_shape=jax.ShapeDtypeStruct((D, 2 * LANES...  54.8 us
    unnamed x1, local copies, waits for them, and re-layouts  1.88 us

commit v1 on v0

--- a/solution.py
+++ b/solution.py
@@ -27,7 +27,7 @@
     return lax.rem(lax.div(y + 1, 2), 2)
 
 
-def gather(k_ref, v_ref, kbuf, vbuf, send, recv, local, meanwhile, later):
+def gather(k_ref, v_ref, kbuf, vbuf, send, recv, local, meanwhile, prepare, later):
     pb, ka = lax.axis_index("pb"), lax.axis_index("ka")
     x, z = lax.div(pb, RING), lax.rem(pb, RING)
     y, c = lax.div(ka, 2), lax.rem(ka, 2)
@@ -137,10 +137,14 @@
                 downward = pass_on(kind, i, hi, down, ring(s + 1))
         coming[kind, i] = (upward, downward)
         for zz in got:
-            if kind == K:
-                to_sibling(kbuf, spot(c, zz, units[i], 0), 2)
-            else:
+            if kind == V:
                 cross_v(zz, units[i])
+            elif i == 1 and s < 4:
+                to_sibling(kbuf, spot(c, zz, 0, 0), 4)
+            elif i == 1:
+                to_sibling(kbuf, spot(c, zz, new_u, 0), 2)
+            elif s == 4:
+                to_sibling(kbuf, spot(c, zz, own_u, 0), 2)
 
     k_cross.wait_recv()
     begin(K, 0)
@@ -149,29 +153,30 @@
     cross_v(z, new_u)
     k_swap.wait_recv()
     advance(V, 0, 1)
-    later()
     k_diagonal.wait_recv()
     begin(K, 1)
     to_sibling(kbuf, spot(c, z, 0, 0), 4)
+    prepare()
     order = ((K, 0, 1), (V, 1, 1), (V, 0, 2), (K, 1, 1), (K, 0, 2), (V, 1, 2), (V, 0, 3), (K, 1, 2), (K, 0, 3), (V, 1, 3),
              (V, 0, 4), (K, 1, 3), (K, 0, 4), (V, 1, 4), (K, 1, 4))
     for kind, i, s in order:
         advance(kind, i, s)
+        if (kind, i, s) == (V, 0, 3):
+            later()
         while len(v_cross) > 4:
             land_v()
     while v_cross:
         land_v()
     for copy in late:
         copy.wait_recv()
-    for copy in started:
-        copy.wait_send()
+    return started
 
 
 COPIES = 80
 
 
 HALF = 512
-CHUNK = 256
+CHUNK = 512
 EXTRA = 16
 UNROLL = 7
 ENTRIES = 40
@@ -234,8 +239,10 @@
     fetch_lists = pltpu.make_async_copy(lvm, lsm, lsem)
     later = fetch_lists.start
 
+    def prepare():
+        write_lists(order_ref, mask_ref, lvm, table, lax.div(y, 2))
+
     def meanwhile():
-        write_lists(order_ref, mask_ref, lvm, table, lax.div(y, 2))
         for s in range(8):
             for i in range(HALF // D):
                 cols = pl.ds(pl.multiple_of(head * LANES + c * HALF + i * D, D), D)
@@ -251,7 +258,7 @@
         acc[0] = jnp.zeros(acc.shape[1:], F32)
         mb[0] = jnp.full(mb.shape[1:], LOW, F32)
 
-    gather(k_ref, v_ref, kbuf, vbuf, send, recv, local, meanwhile, later)
+    gathered = gather(k_ref, v_ref, kbuf, vbuf, send, recv, local, meanwhile, prepare, later)
     fetch_lists.wait()
     for copy in fetch:
         copy.wait()
@@ -315,8 +322,10 @@
         src, dst = kinds[kind]
         return pltpu.make_async_copy(src.at[6 + c], dst.at[y, c], near_sem.at[kind])
 
+    second, third = jnp.where(c == 0, nearby, partner), jnp.where(c == 0, partner, nearby)
+
     def pair_of(phase):
-        return jnp.where(phase == 0, far, jnp.where(phase == 1, nearby, jnp.where(phase == 2, partner, y)))
+        return jnp.where(phase == 0, far, jnp.where(phase == 1, second, jnp.where(phase == 2, third, y)))
 
     def run_phase(phase, _):
         p = pair_of(phase)
@@ -369,6 +378,8 @@
                 both = land[a, core, :, cut].astype(F32) * fa[:, cut] + land[b, core, :, cut].astype(F32) * fb[:, cut]
                 at = pl.multiple_of(kv * LANES + core * HALF + i * D, D)
                 out_ref[:, pl.ds(at, D)] = both.T.astype(BF16)
+    for copy in gathered:
+        copy.wait_send()
     for phase in range(4):
         for j in range(2):
             for kind in range(2):

time: 56.8 us -> 55.9 us (0.984)
  Pallas kernels: 54.8 us -> 53.8 us
    pallas_call x1, Pallas kernels: 54.8 us -> 53.8 us  [fused(): pl.pallas_call(fused_kernel, out_shape=jax.ShapeDtypeStruct((D, 2 * LANES...]
where the time goes in v1:
time: 55.9 us; the launch traced here: 55.7 us
  Pallas kernels  53.8 us (96%)
  local copies, waits for them, and re-layouts  1.88 us (3%)
    pallas_call x1, Pallas kernels, fused(): pl.pallas_call(fused_kernel, out_shape=jax.ShapeDtypeStruct((D, 2 * LANES...  53.8 us
    unnamed x1, local copies, waits for them, and re-layouts  1.88 us

profile of v1, /device:TPU:1, one launch (start us, length us, event | category | flops | bytes accessed | tf_op | source)
XLA Modules:
  0.0 55.7 jit_solution(5925234502022352668)
XLA Ops:
  0.0 53.8 %attend_all.1 = bf16[128,2048]{1,0:T(8,128)(2,1)} custom-call(s32[8]{0:T(128)} %order_ref.1, s32[8,128]{1,0:T(8,128)} %mask_ref.1, bf16[1024,2048]{1,0:T(8,128)(2,1)} %q_hbm.1, bf16[128,256]{1,0:T(8,128)(2,1)} %bitcast.2, bf16[128,256]{1,0:T(8,128)(2,1)} %bitcast.3), custom_call_target="tpu_custom_call" | custom-call | tf_op jit(solution)/shard_map/attend_all/pallas_call | solution.py:397
  53.8 1.9 %copy.7 = bf16[128,2048]{1,0:T(8,128)(2,1)} copy(bf16[128,2048]{1,0:T(8,128)(2,1)} %attend_all.1) | data formatting | bytes 1048576

commit v2 on v1

--- a/solution.py
+++ b/solution.py
@@ -178,7 +178,6 @@
 HALF = 512
 CHUNK = 512
 EXTRA = 16
-UNROLL = 7
 ENTRIES = 40
 
 
@@ -283,7 +282,7 @@
         pads = [e >= 2 * POOL for e in listed]
         v = jnp.concatenate([vbuf[e & (POOL - 1)] for e in listed], axis=0)
         vt = jnp.concatenate([v.T, ones], axis=0)
-        now, then = lax.rem(jnp.int32(g), 2), lax.rem(jnp.int32(g) + 1, 2)
+        now, then = g % 2, (g + 1) % 2
         for w in range(0, HALF, CHUNK):
             cut = slice(w, w + CHUNK)
             pieces = [sb[now, k * D:(k + 1) * D, cut] for k in range(WIDE)]
@@ -333,12 +332,8 @@
             sb[0, :, w:w + CHUNK] = scores(p, 0, w)
         stage(p, 0, 0)
 
-        def step(i, _):
-            for t in range(UNROLL):
-                stage(p, 1 + i * UNROLL + t, None)
-            return 0
-
-        lax.fori_loop(0, (NG - 2) // UNROLL, step, 0)
+        for g in range(1, NG - 1):
+            stage(p, g, None)
         stage(p, NG - 1, WIDE - 1, more=False)
         for j in range(2):
             at = split(p) if j == 0 else NG
@@ -377,7 +372,7 @@
                 cut = slice(i * D, (i + 1) * D)
                 both = land[a, core, :, cut].astype(F32) * fa[:, cut] + land[b, core, :, cut].astype(F32) * fb[:, cut]
                 at = pl.multiple_of(kv * LANES + core * HALF + i * D, D)
-                out_ref[:, pl.ds(at, D)] = both.T.astype(BF16)
+                out_ref[:, pl.ds(at, D)] = both.astype(BF16).T
     for copy in gathered:
         copy.wait_send()
     for phase in range(4):
@@ -411,9 +406,9 @@
             pltpu.VMEM((NG + 1, 8, HALF), F32),
             pltpu.VMEM((2, WIDE * D, HALF), F32),
             pltpu.VMEM((8, D, HALF), BF16),
-            pltpu.VMEM((8, 8, HALF), F32),
+            pltpu.VMEM((8, 2, HALF), F32),
             pltpu.VMEM((4, 2, D, HALF), BF16),
-            pltpu.VMEM((4, 2, 8, HALF), F32),
+            pltpu.VMEM((4, 2, 2, HALF), F32),
             dma((COPIES,)), dma((COPIES,)), dma((2,)), dma(()), dma((8 * HALF // D,)),
             dma((8, 2)), dma((4, 2, 2)), dma((2,)),
         ],

time: 55.9 us -> 54.8 us (0.980)
  Pallas kernels: 53.8 us -> 52.7 us
    pallas_call x1, Pallas kernels: 53.8 us -> 52.7 us  [fused(): pl.pallas_call(fused_kernel, out_shape=jax.ShapeDtypeStruct((D, 2 * LANES...]
where the time goes in v2:
time: 54.8 us; the launch traced here: 54.6 us
  Pallas kernels  52.7 us (96%)
  local copies, waits for them, and re-layouts  1.88 us (3%)
    pallas_call x1, Pallas kernels, fused(): pl.pallas_call(fused_kernel, out_shape=jax.ShapeDtypeStruct((D, 2 * LANES...  52.7 us
    unnamed x1, local copies, waits for them, and re-layouts  1.88 us

profile of v2, /device:TPU:1, one launch (start us, length us, event | category | flops | bytes accessed | tf_op | source)
XLA Modules:
  0.0 54.6 jit_solution(16212701437337815045)
XLA Ops:
  0.0 52.7 %attend_all.1 = bf16[128,2048]{1,0:T(8,128)(2,1)} custom-call(s32[8]{0:T(128)} %order_ref.1, s32[8,128]{1,0:T(8,128)} %mask_ref.1, bf16[1024,2048]{1,0:T(8,128)(2,1)} %q_hbm.1, bf16[128,256]{1,0:T(8,128)(2,1)} %bitcast.2, bf16[128,256]{1,0:T(8,128)(2,1)} %bitcast.3), custom_call_target="tpu_custom_call" | custom-call | tf_op jit(solution)/shard_map/attend_all/pallas_call | solution.py:392
  52.7 1.9 %copy.7 = bf16[128,2048]{1,0:T(8,128)(2,1)} copy(bf16[128,2048]{1,0:T(8,128)(2,1)} %attend_all.1) | data formatting | bytes 1048576
